TPU v7x, 32 devices: a whole 2x2x4 slice. The times are simulated.
32 devices in a mesh: dp: 8 (over z, x), tensor: 4 (over y, core).
Axes of the slice: x: 2, y: 2, z: 4, core: 2. Of those that a mesh axis runs over, the one named last changes fastest.
Arguments:
- tokens: bfloat16 [32768, 768], P(('dp', 'tensor')), may hold values from -6 to 6
- cotangent: bfloat16 [32768, 768], P(('dp', 'tensor')), may hold values from -26 to 26
- seq_group: int32 [16], P('dp'), may hold values from 0 to 1
- block_slot: int32 [13830], replicated, may hold values from 0 to 20751, as said below
- master: float32 [4, 20752, 128], P('tensor', 'dp'), may hold values from -3 to 3
- first_moment: float32 [4, 20752, 128], P('tensor', 'dp'), may hold values from -1 to 1
- second_moment: float32 [4, 20752, 128], P('tensor', 'dp'), may hold values from 0 to 1, as said below
Outputs:
- output: bfloat16 [32768, 768], P(('dp', 'tensor'))
- input_grad: float32 [32768, 768], P(('dp', 'tensor'))
- group_norms: float32 [16], P('dp')
- new_master: float32 [4, 20752, 128], P('tensor', 'dp')
- new_first: float32 [4, 20752, 128], P('tensor', 'dp')
- new_second: float32 [4, 20752, 128], P('tensor', 'dp')
Inputs may be any that keep to these rules, and one draw needn't show every extreme that they name: `block_slot`: all entries differ; slot s belongs to the owner with dp index s // 2594; one owner holds 2594 blocks. `seq_group`: group ids count within one dp index: sequences of different dp indices never share a group. `second_moment`: Positive.
All inputs are finite; a program needn't handle non-finite values.
Results may differ from a plain program's by a relative error of at most 0.012.
Values may be sent and summed in bfloat16 or wider, within the bound.
No kernel may reach another device: no remote copies, remote signals or barrier semaphores. Data moves between devices by JAX's collectives and lax.ppermute only.
A program may use at most 256 MiB of HBM per device.

v0:
```python
import jax
import jax.numpy as jnp
from jax import lax
from jax.sharding import PartitionSpec as P

HEADS = 12
HD = 64
ROT = 16
FF = 3072
eps_norm = 1e-05
eps_adam = 1e-08
beta_one = 0.5
beta_two = 0.6
root_half = 0.7071067811865476
inv_root_tau = 0.3989422804014327


def rotary_tables(length, rot_dims):
    half_rot = rot_dims // 2
    frequency = 10000.0 ** (-2.0 * jnp.arange(half_rot, dtype=jnp.float32) / rot_dims)
    angles = jnp.arange(length, dtype=jnp.float32)[:, None] * frequency[None, :]
    return (jnp.cos(angles), jnp.sin(angles))


def rotate(features, cosine, sine_table, rot_dims):
    half_rot = rot_dims // 2
    first_half = features[..., :half_rot]
    second_half = features[..., half_rot:rot_dims]
    cos_cols = cosine[:, None, :]
    sin_cols = sine_table[:, None, :]
    return jnp.concatenate(
        [
            first_half * cos_cols - second_half * sin_cols,
            second_half * cos_cols + first_half * sin_cols,
            features[..., rot_dims:],
        ],
        axis=-1,
    )


def unrotate(grad_in, cosine, sine_table, rot_dims):
    half_rot = rot_dims // 2
    first_half = grad_in[..., :half_rot]
    second_half = grad_in[..., half_rot:rot_dims]
    cos_cols = cosine[:, None, :]
    sin_cols = sine_table[:, None, :]
    return jnp.concatenate(
        [
            first_half * cos_cols + second_half * sin_cols,
            second_half * cos_cols - first_half * sin_cols,
            grad_in[..., rot_dims:],
        ],
        axis=-1,
    )


def layer_norm(rows_in):
    row_mean = jnp.mean(rows_in, axis=-1, keepdims=True)
    centred = rows_in - row_mean
    inverse = lax.rsqrt(jnp.mean(centred * centred, axis=-1, keepdims=True) + eps_norm)
    return (centred * inverse, inverse)


def unpack(flat_params, d_model, heads_local, ff_local, width_local):
    inner_width = heads_local * HD
    end_qkv = d_model * 3 * inner_width
    end_out = end_qkv + inner_width * d_model
    end_up = end_out + d_model * ff_local
    end_down = end_up + ff_local * d_model
    return (
        flat_params[:end_qkv].reshape(d_model, 3 * inner_width),
        flat_params[end_qkv:end_out].reshape(inner_width, d_model),
        flat_params[end_out:end_up].reshape(d_model, ff_local),
        flat_params[end_up:end_down].reshape(ff_local, d_model),
        flat_params[end_down:].reshape(4, width_local),
    )


def step_rates(position, d_model, heads_local, head_dim, ff_local, seq_len, ff_all):
    end_qkv = d_model * 3 * heads_local * head_dim
    end_out = end_qkv + heads_local * head_dim * d_model
    end_up = end_out + d_model * ff_local
    end_down = end_up + ff_local * d_model
    matrix_rate = d_model ** (-0.5)
    learn_rate = jnp.where(
        position < end_qkv,
        matrix_rate,
        jnp.where(
            position < end_out,
            (seq_len / (5.0 * d_model)) ** 0.5,
            jnp.where(
                position < end_up,
                matrix_rate,
                jnp.where(position < end_down, ff_all ** (-0.5), 0.1),
            ),
        ),
    )
    weight_decay = jnp.where(position < end_down, 0.1, 0.0)
    return (learn_rate.astype(jnp.float32), weight_decay.astype(jnp.float32))


def adam_update(weight, moment_one, moment_two, gradient, learn_rate, weight_decay):
    new_one = beta_one * moment_one + (1.0 - beta_one) * gradient
    new_two = beta_two * moment_two + (1.0 - beta_two) * gradient * gradient
    new_weight = weight - learn_rate * (
        new_one / (jnp.sqrt(new_two) + eps_adam) + weight_decay * weight
    )
    return (new_weight, new_one, new_two)


def by_sequence(tensor_in, seq_count):
    return tensor_in.reshape(seq_count, -1, tensor_in.shape[-1])


def seq_product(left, right, seq_count):
    return jnp.einsum(
        "sli,slj->sij",
        by_sequence(left, seq_count),
        by_sequence(right, seq_count),
        preferred_element_type=jnp.float32,
    )


def on_device(tokens, cotangent, seq_group, block_slot, master, first_moment, second_moment):
    tensor_count = lax.axis_size("tensor")
    tensor_rank = lax.axis_index("tensor")
    owner_index = lax.axis_index("dp")
    owner_count = lax.axis_size("dp")
    d_model = tokens.shape[1]
    local_rows = tokens.shape[0]
    width_local = d_model // tensor_count
    heads_local = HEADS // tensor_count
    inner_width = heads_local * HD
    ff_local = FF // tensor_count
    seq_count = seq_group.shape[0]
    tok_count = local_rows * tensor_count
    seq_len = tok_count // seq_count
    capacity = master.shape[1]
    block_width = master.shape[2]
    block_count = block_slot.shape[0]
    copies = lax.all_gather(master[0].astype(jnp.bfloat16), "dp", axis=0, tiled=True)
    flat_params = copies[block_slot].reshape(-1)
    w_qkv, w_out, w_up, w_down, norm_local = unpack(
        flat_params, d_model, heads_local, ff_local, width_local
    )
    x_full, norm_rows = (
        lax.all_gather(tokens, "tensor", axis=0, tiled=True),
        lax.all_gather(norm_local.reshape(1, 4 * width_local), "tensor", axis=0, tiled=True),
    )
    norm_full = jnp.transpose(norm_rows.reshape(tensor_count, 4, width_local), (1, 0, 2)).reshape(
        4, d_model
    )
    rows_full = x_full.astype(jnp.float32)
    normed, inverse = layer_norm(rows_full)
    norm_gains = norm_full.astype(jnp.float32)
    first_in = (normed * norm_gains[0] + norm_gains[1]).astype(jnp.bfloat16)
    second_in = (normed * norm_gains[2] + norm_gains[3]).astype(jnp.bfloat16)
    projected = jnp.dot(first_in, w_qkv, preferred_element_type=jnp.float32).reshape(
        seq_count, seq_len, 3, heads_local, HD
    )
    cosine, sine_table = rotary_tables(seq_len, ROT)
    queries = rotate(projected[:, :, 0], cosine, sine_table, ROT).astype(jnp.bfloat16)
    key_rows = rotate(projected[:, :, 1], cosine, sine_table, ROT).astype(jnp.bfloat16)
    values = projected[:, :, 2].astype(jnp.bfloat16)
    block_rows = min(512, seq_len)
    block_total = seq_len // block_rows
    scale_factor = HD ** (-0.5)
    starts = jnp.arange(block_total, dtype=jnp.int32) * block_rows
    key_index = jnp.arange(seq_len, dtype=jnp.int32)

    def scores_of(row_start):
        query_block = lax.dynamic_slice_in_dim(queries, row_start, block_rows, 1)
        scores = (
            jnp.einsum("sqhd,skhd->shqk", query_block, key_rows, preferred_element_type=jnp.float32)
            * scale_factor
        )
        allowed = (row_start + jnp.arange(block_rows, dtype=jnp.int32))[:, None] >= key_index[
            None, :
        ]
        return (jnp.where(allowed, scores, -1e30), query_block)

    def forward_block(row_start):
        scores = scores_of(row_start)[0]
        row_peak = jnp.max(scores, axis=-1, keepdims=True)
        exp_scores = jnp.exp(scores - row_peak)
        row_total = jnp.sum(exp_scores, axis=-1, keepdims=True)
        weights_low = (exp_scores / row_total).astype(jnp.bfloat16)
        mixed_heads = jnp.einsum(
            "shqk,skhd->sqhd", weights_low, values, preferred_element_type=jnp.float32
        )
        return (mixed_heads, row_peak + jnp.log(row_total))

    mixed_heads, log_sums = lax.map(forward_block, starts)
    attended = jnp.moveaxis(mixed_heads, 0, 1).reshape(tok_count, inner_width).astype(jnp.bfloat16)
    hidden_pre = jnp.dot(second_in, w_up, preferred_element_type=jnp.float32)
    hidden_low = jax.nn.gelu(hidden_pre, approximate=False).astype(jnp.bfloat16)
    branch = jnp.dot(attended, w_out, preferred_element_type=jnp.float32) + jnp.dot(
        hidden_low, w_down, preferred_element_type=jnp.float32
    )
    branch_sum = lax.psum_scatter(
        branch.astype(jnp.bfloat16), "tensor", scatter_dimension=0, tiled=True
    ).astype(jnp.float32)
    output = (tokens.astype(jnp.float32) + branch_sum).astype(jnp.bfloat16)
    back_full = lax.all_gather(cotangent, "tensor", axis=0, tiled=True)
    grad_down = seq_product(hidden_low, back_full, seq_count)
    grad_hidden = jnp.dot(back_full, w_down.T, preferred_element_type=jnp.float32)
    cumulative = 0.5 * (1.0 + lax.erf(hidden_pre * root_half))
    density = jnp.exp(-0.5 * hidden_pre * hidden_pre) * inv_root_tau
    grad_pre = (grad_hidden * (cumulative + hidden_pre * density)).astype(jnp.bfloat16)
    grad_up = seq_product(second_in, grad_pre, seq_count)
    second_back = jnp.dot(grad_pre, w_up.T, preferred_element_type=jnp.float32)
    grad_out = seq_product(attended, back_full, seq_count)
    grad_attended = jnp.dot(back_full, w_out.T, preferred_element_type=jnp.float32).astype(
        jnp.bfloat16
    )
    grad_blocks_in = jnp.moveaxis(
        grad_attended.reshape(seq_count, block_total, block_rows, heads_local, HD), 1, 0
    )

    def backward_block(carried, inputs):
        row_start, log_sum, grad_block = inputs
        scores, query_block = scores_of(row_start)
        probs = jnp.exp(scores - log_sum)
        grad_probs = jnp.einsum(
            "sqhd,skhd->shqk", grad_block, values, preferred_element_type=jnp.float32
        )
        row_dot = jnp.sum(probs * grad_probs, axis=-1, keepdims=True)
        grad_scores = (probs * (grad_probs - row_dot)).astype(jnp.bfloat16)
        grad_query = (
            jnp.einsum("shqk,skhd->sqhd", grad_scores, key_rows, preferred_element_type=jnp.float32)
            * scale_factor
        )
        grad_keys = (
            carried[0]
            + jnp.einsum(
                "shqk,sqhd->skhd", grad_scores, query_block, preferred_element_type=jnp.float32
            )
            * scale_factor
        )
        grad_values = carried[1] + jnp.einsum(
            "shqk,sqhd->skhd",
            probs.astype(jnp.bfloat16),
            grad_block,
            preferred_element_type=jnp.float32,
        )
        return ((grad_keys, grad_values), grad_query)

    zero_heads = jnp.zeros((seq_count, seq_len, heads_local, HD), jnp.float32)
    key_value_grads, grad_queries = lax.scan(
        backward_block, (zero_heads, zero_heads), (starts, log_sums, grad_blocks_in)
    )
    grad_queries = jnp.moveaxis(grad_queries, 0, 1).reshape(seq_count, seq_len, heads_local, HD)
    grad_qkv = (
        jnp.stack(
            [
                unrotate(grad_queries, cosine, sine_table, ROT),
                unrotate(key_value_grads[0], cosine, sine_table, ROT),
                key_value_grads[1],
            ],
            axis=2,
        )
        .reshape(tok_count, 3 * inner_width)
        .astype(jnp.bfloat16)
    )
    grad_qkv_w = seq_product(first_in, grad_qkv, seq_count)
    first_back = jnp.dot(grad_qkv, w_qkv.T, preferred_element_type=jnp.float32)
    row_start_local = tensor_rank * local_rows
    first_sum, second_sum = (
        lax.psum_scatter(
            first_back.astype(jnp.bfloat16), "tensor", scatter_dimension=0, tiled=True
        ).astype(jnp.float32),
        lax.psum_scatter(
            second_back.astype(jnp.bfloat16), "tensor", scatter_dimension=0, tiled=True
        ).astype(jnp.float32),
    )
    normed_rows = lax.dynamic_slice_in_dim(normed, row_start_local, local_rows, 0)
    inverse_rows = lax.dynamic_slice_in_dim(inverse, row_start_local, local_rows, 0)
    scaled_first = first_sum * norm_gains[0]
    scaled_second = second_sum * norm_gains[2]
    first_mean = jnp.mean(scaled_first, axis=1, keepdims=True)
    first_cross = jnp.mean(scaled_first * normed_rows, axis=1, keepdims=True)
    second_mean = jnp.mean(scaled_second, axis=1, keepdims=True)
    second_cross = jnp.mean(scaled_second * normed_rows, axis=1, keepdims=True)
    grad_input = (
        cotangent.astype(jnp.float32)
        + inverse_rows * (scaled_first - first_mean - normed_rows * first_cross)
        + inverse_rows * (scaled_second - second_mean - normed_rows * second_cross)
    )
    row_seq = (row_start_local + jnp.arange(local_rows, dtype=jnp.int32)) // seq_len
    row_member = (row_seq[None, :] == jnp.arange(seq_count, dtype=jnp.int32)[:, None]).astype(
        jnp.float32
    )
    partial_sums = jnp.stack(
        [
            jnp.dot(row_member, first_sum * normed_rows, precision=lax.Precision.HIGHEST),
            jnp.dot(row_member, first_sum, precision=lax.Precision.HIGHEST),
            jnp.dot(row_member, second_sum * normed_rows, precision=lax.Precision.HIGHEST),
            jnp.dot(row_member, second_sum, precision=lax.Precision.HIGHEST),
        ],
        axis=1,
    )
    norm_grads = lax.psum_scatter(partial_sums, "tensor", scatter_dimension=2, tiled=True)
    per_seq = jnp.concatenate(
        [
            grad_qkv_w.reshape(seq_count, -1),
            grad_out.reshape(seq_count, -1),
            grad_up.reshape(seq_count, -1),
            grad_down.reshape(seq_count, -1),
            norm_grads.reshape(seq_count, -1),
        ],
        axis=1,
    )
    member = (seq_group[None, :] == jnp.arange(seq_count, dtype=jnp.int32)[:, None]).astype(
        jnp.float32
    )
    group_grads = jnp.dot(member, per_seq, precision=lax.Precision.HIGHEST)
    squares = lax.psum(jnp.sum(group_grads * group_grads, axis=1), "tensor")
    group_norms = jnp.sqrt(squares)
    clip_scale = 1.0 / jnp.maximum(group_norms, 1.0)
    clipped = jnp.dot(clip_scale, group_grads, precision=lax.Precision.HIGHEST)
    grad_rows = clipped.reshape(block_count, block_width)
    slot_total = owner_count * capacity
    slot_block = (
        jnp.full((slot_total,), -1, jnp.int32)
        .at[block_slot]
        .set(jnp.arange(block_count, dtype=jnp.int32))
    )
    my_blocks = lax.dynamic_slice_in_dim(slot_block, owner_index * capacity, capacity)
    summed = lax.psum(grad_rows, "dp")
    owned_grad = jnp.where(my_blocks[:, None] >= 0, summed[jnp.maximum(my_blocks, 0)], 0.0)
    position = (
        jnp.maximum(my_blocks, 0)[:, None] * block_width
        + jnp.arange(block_width, dtype=jnp.int32)[None, :]
    )
    learn_rate, weight_decay = step_rates(position, d_model, heads_local, HD, ff_local, seq_len, FF)
    new_weight, new_one, new_two = adam_update(
        master[0], first_moment[0], second_moment[0], owned_grad, learn_rate, weight_decay
    )
    return (output, grad_input, group_norms, new_weight[None], new_one[None], new_two[None])


def solution(mesh):
    placed = (
        P(("dp", "tensor"), None),
        P(("dp", "tensor"), None),
        P("dp"),
        P(),
        P("tensor", "dp", None),
        P("tensor", "dp", None),
        P("tensor", "dp", None),
    )
    return jax.shard_map(
        on_device,
        mesh=mesh,
        in_specs=placed,
        out_specs=(
            P(("dp", "tensor"), None),
            P(("dp", "tensor"), None),
            P("dp"),
            P("tensor", "dp", None),
            P("tensor", "dp", None),
            P("tensor", "dp", None),
        ),
        check_vma=False,
    )
```

profile of v0, /device:TPU:0, one launch (start us, length us, event | category | flops | bytes accessed | tf_op | source)
XLA Modules:
  0.0 1451.3 jit_solution(10674566761597092681)
XLA Ops:
  17.1 148.8 %all-gather.10.cloned.1.call-done = bf16[1,20752,128]{2,0,1:T(2,128)(2,1)} async-done(((bf16[1,2594,128]{2,0,1:T(2,128)(2,1)}), bf16[1,20752,128]{2,0,1:T(2,128)(2,1)}) %all-gather.10.cloned.1.call-update) | async-done | bytes 5312528 | tf_op jit(solution)/shard_map/all_gather | solution.py:141
  165.9 8.5 copy.115
  174.4 30.7 %gather_fusion = bf16[13830,128]{1,0:T(8,128)(2,1)S(1)} fusion(bf16[20752,128]{1,0:T(8,128)(2,1)} %bitcast.203, s32[14336]{0:T(1024)} %pad_clamp_fusion), kind=kCustom, calls=%fused_computation | custom fusion | bytes 7136280 | tf_op jit(solution)/shard_map/gather | solution.py:142
  234.9 7.9 fusion.36
  250.1 10.0 all-gather.8.cloned.1.call-done
  260.0 6.1 fusion.55
  276.1 163.2 %while.30 = (s32[]{:T(128)}, bf16[4,2,512,3,64]{2,4,3,1,0:T(8,128)(2,1)}, f32[4,2,3,512,1]{3,2,1,4,0:T(4,128)S(1)}, s32[4]{0:T(128)S(1)}, bf16[2,2048,3,64]{1,3,...) while((s32[]{:T(128)}, ...), condition=%wide.region_5.6_spmd.clone.clone, body=%wide.region_2.5_spmd.clone.sunk.clone | while | flops 1687156224 | bytes 96723152 | solution.py:193
  280.0 12.1 fusion.178
  292.1 12.1 fusion.179
  304.2 11.6 fusion.180
  320.8 12.1 fusion.178
  332.9 12.1 fusion.179
  345.0 11.6 fusion.180
  361.6 12.1 fusion.178
  373.7 12.1 fusion.179
  385.8 11.6 fusion.180
  402.4 12.1 fusion.178
  414.5 12.1 fusion.179
  426.6 11.6 fusion.180
  439.3 336.2 %while.31 = (s32[]{:T(128)}, f32[2,2048,3,64]{1,3,2,0:T(8,128)}, f32[2,2048,3,64]{1,3,2,0:T(8,128)}, f32[4,2,512,3,64]{2,4,3,1,0:T(8,128)}, s32[4]{0:T(128)S(1)}...) while((s32[]{:T(128)}, f32[2,2048,3,64]{1,3,2,0:T(8,128)}, ...), condition=%wide.region_9.10_spmd.clone.clone, body=%wide.region_7.9_spmd.clone.sunk.clone | while | flops 4126078464 | bytes 275603712 | solution.py:249
  443.5 11.3 fusion.190
  454.8 12.9 bitcast_add_fusion.7
  467.7 18.1 %multiply_reduce_fusion.4 = (f32[2,3,512]{2,1,0:T(4,128)S(1)}, f32[2,3,512,2048]{3,2,1,0:T(8,128)}) fusion(f32[2,3,512,2048]{3,2,1,0:T(8,128)} %fusion.190, f32[2,3,512]{2,1,0:T(4,128)S(1)} %dynamic-slice_bitcast_fusion.3, pred[512,2048]{1,0:T(8,128)(4,1)S(1)} %iota_compare_fusion.12, bf16[2,2048,3,64]{1,3,2,0:T(8,128)(2,1)} %copy-done.1, ...), kind=kOutput, calls=%fused_computation.22.clone.1.clone | convolution fusion | flops 836760576 | bytes 53370884 | tf_op jit(solution)/shard_map/while/body/eval_jaxpr/sqhd,skhd->shqk/dot_general | solution.py:224
  485.8 17.0 %multiply_convert_fusion.3 = bf16[2,3,512,2048]{3,2,1,0:T(8,128)(2,1)S(1)} fusion(f32[2,3,512,2048]{3,2,1,0:T(8,128)} %get-tuple-element.409, f32[2,3,512,2048]{3,2,1,0:T(8,128)} %fusion.190, f32[2,3,512]{2,1,0:T(4,128)S(1)} %get-tuple-element.410, f32[2,3,512]{2,1,0:T(4,128)S(1)} %dynamic-slice_bitcast_fusion.3, ...), kind=kLoop, calls=%fused_computation.21.clone.1.clone | loop fusion | flops 37748736 | bytes 63987712 | tf_op jit(solution)/shard_map/while/body/eval_jaxpr/convert_element_type | solution.py:228
  512.5 9.5 fusion.191
  526.0 11.3 fusion.190
  537.3 13.8 bitcast_add_fusion.7
  551.1 18.1 %multiply_reduce_fusion.4 = (f32[2,3,512]{2,1,0:T(4,128)S(1)}, f32[2,3,512,2048]{3,2,1,0:T(8,128)}) fusion(f32[2,3,512,2048]{3,2,1,0:T(8,128)} %fusion.190, f32[2,3,512]{2,1,0:T(4,128)S(1)} %dynamic-slice_bitcast_fusion.3, pred[512,2048]{1,0:T(8,128)(4,1)S(1)} %iota_compare_fusion.12, bf16[2,2048,3,64]{1,3,2,0:T(8,128)(2,1)} %copy-done.1, ...), kind=kOutput, calls=%fused_computation.22.clone.1.clone | convolution fusion | flops 836760576 | bytes 53370884 | tf_op jit(solution)/shard_map/while/body/eval_jaxpr/sqhd,skhd->shqk/dot_general | solution.py:224
  569.2 17.0 %multiply_convert_fusion.3 = bf16[2,3,512,2048]{3,2,1,0:T(8,128)(2,1)S(1)} fusion(f32[2,3,512,2048]{3,2,1,0:T(8,128)} %get-tuple-element.409, f32[2,3,512,2048]{3,2,1,0:T(8,128)} %fusion.190, f32[2,3,512]{2,1,0:T(4,128)S(1)} %get-tuple-element.410, f32[2,3,512]{2,1,0:T(4,128)S(1)} %dynamic-slice_bitcast_fusion.3, ...), kind=kLoop, calls=%fused_computation.21.clone.1.clone | loop fusion | flops 37748736 | bytes 63987712 | tf_op jit(solution)/shard_map/while/body/eval_jaxpr/convert_element_type | solution.py:228
  590.8 6.1 bitcast_add_fusion.6
  596.9 9.5 fusion.191
  610.4 11.3 fusion.190
  621.7 13.8 bitcast_add_fusion.7
  635.5 18.1 %multiply_reduce_fusion.4 = (f32[2,3,512]{2,1,0:T(4,128)S(1)}, f32[2,3,512,2048]{3,2,1,0:T(8,128)}) fusion(f32[2,3,512,2048]{3,2,1,0:T(8,128)} %fusion.190, f32[2,3,512]{2,1,0:T(4,128)S(1)} %dynamic-slice_bitcast_fusion.3, pred[512,2048]{1,0:T(8,128)(4,1)S(1)} %iota_compare_fusion.12, bf16[2,2048,3,64]{1,3,2,0:T(8,128)(2,1)} %copy-done.1, ...), kind=kOutput, calls=%fused_computation.22.clone.1.clone | convolution fusion | flops 836760576 | bytes 53370884 | tf_op jit(solution)/shard_map/while/body/eval_jaxpr/sqhd,skhd->shqk/dot_general | solution.py:224
  653.6 17.0 %multiply_convert_fusion.3 = bf16[2,3,512,2048]{3,2,1,0:T(8,128)(2,1)S(1)} fusion(f32[2,3,512,2048]{3,2,1,0:T(8,128)} %get-tuple-element.409, f32[2,3,512,2048]{3,2,1,0:T(8,128)} %fusion.190, f32[2,3,512]{2,1,0:T(4,128)S(1)} %get-tuple-element.410, f32[2,3,512]{2,1,0:T(4,128)S(1)} %dynamic-slice_bitcast_fusion.3, ...), kind=kLoop, calls=%fused_computation.21.clone.1.clone | loop fusion | flops 37748736 | bytes 63987712 | tf_op jit(solution)/shard_map/while/body/eval_jaxpr/convert_element_type | solution.py:228
  675.2 6.1 bitcast_add_fusion.6
  681.3 9.5 fusion.191
  694.8 11.3 fusion.190
  706.1 13.8 bitcast_add_fusion.7
  719.9 18.1 %multiply_reduce_fusion.4 = (f32[2,3,512]{2,1,0:T(4,128)S(1)}, f32[2,3,512,2048]{3,2,1,0:T(8,128)}) fusion(f32[2,3,512,2048]{3,2,1,0:T(8,128)} %fusion.190, f32[2,3,512]{2,1,0:T(4,128)S(1)} %dynamic-slice_bitcast_fusion.3, pred[512,2048]{1,0:T(8,128)(4,1)S(1)} %iota_compare_fusion.12, bf16[2,2048,3,64]{1,3,2,0:T(8,128)(2,1)} %copy-done.1, ...), kind=kOutput, calls=%fused_computation.22.clone.1.clone | convolution fusion | flops 836760576 | bytes 53370884 | tf_op jit(solution)/shard_map/while/body/eval_jaxpr/sqhd,skhd->shqk/dot_general | solution.py:224
  738.0 17.0 %multiply_convert_fusion.3 = bf16[2,3,512,2048]{3,2,1,0:T(8,128)(2,1)S(1)} fusion(f32[2,3,512,2048]{3,2,1,0:T(8,128)} %get-tuple-element.409, f32[2,3,512,2048]{3,2,1,0:T(8,128)} %fusion.190, f32[2,3,512]{2,1,0:T(4,128)S(1)} %get-tuple-element.410, f32[2,3,512]{2,1,0:T(4,128)S(1)} %dynamic-slice_bitcast_fusion.3, ...), kind=kLoop, calls=%fused_computation.21.clone.1.clone | loop fusion | flops 37748736 | bytes 63987712 | tf_op jit(solution)/shard_map/while/body/eval_jaxpr/convert_element_type | solution.py:228
  765.7 9.5 fusion.191
  788.4 9.5 copy.74
  813.7 9.7 fusion.108
  828.9 9.4 convolution_convert_fusion
  840.7 33.3 %fusion.41 = (bf16[4096,768]{1,0:T(8,128)(2,1)}, f32[4096,768]{1,0:T(8,128)S(1)}) fusion(bf16[4096,768]{1,0:T(8,128)(2,1)} %get-tuple-element.243, bf16[768,768]{1,0:T(8,128)(2,1)S(1)} %copy-done.22), kind=kOutput, calls=%fused_computation.59 | convolution fusion | flops 5036310528 | bytes 26345472 | tf_op jit(solution)/shard_map/dot_general | solution.py:195
  874.0 9.2 fusion.47
  885.8 7.0 convolution_convert_fusion.1
  892.8 9.4 convolution_bitcast_fusion.1
  909.1 6.2 constant_dynamic-update-slice_fusion.2
  917.7 12.2 convolution_bitcast_fusion
  929.9 11.5 fusion.107
  946.8 21.3 %reduce-scatter.11.cloned.1.call-done = bf16[1024,768]{1,0:T(8,128)(2,1)} async-done(((bf16[4096,768]{1,0:T(8,128)(2,1)}), bf16[1024,768]{1,0:T(8,128)(2,1)}) %reduce-scatter.11.cloned.1.call-update) | async-done | bytes 1572880 | tf_op jit(solution)/shard_map/reduce_scatter | solution.py:272
  977.0 9.1 add_convert_fusion
  986.1 8.1 copy.103
  1002.3 41.5 %multiply_reduce_fusion.1 = (f32[2]{0:T(128)S(1)}, f32[2,1770240]{1,0:T(2,128)}) fusion(f32[2,1770240]{1,0:T(2,128)} %constant_dynamic-update-slice_fusion, s32[2]{0:T(128)S(1)} %copy-done.37), kind=kOutput, calls=%fused_computation.55 | convolution fusion | flops 92052480 | bytes 28323856 | tf_op jit(solution)/shard_map/dot_general | solution.py:316
  1043.8 6.4 psum.14
  1050.1 119.3 %convolution_reduce_fusion = f32[1770240]{0:T(1024)} fusion(f32[2,1770240]{1,0:T(2,128)} %get-tuple-element.263, f32[2]{0:T(128)S(1)} %sqrt.7), kind=kOutput, calls=%fused_computation.116 | convolution fusion | flops 42485764 | bytes 21242888 | tf_op jit(solution)/shard_map/dot_general | solution.py:320
  1169.4 65.6 %scatter_custom_fusion = s32[20752]{0:T(1024)S(1)} fusion(s32[13830]{0:T(1024)} %copy-done.27, s32[13830]{0:T(1024)S(1)} %iota.92, s32[]{:T(128)} %constant.72.clone.1), kind=kCustom, calls=%fused_computation.158 | custom fusion | bytes 83520 | tf_op jit(solution)/shard_map/scatter | solution.py:326
  1246.7 157.5 %all-reduce.2.cloned.1.call-done = f32[13830,128]{1,0:T(8,128)} async-done(((f32[13830,128]{1,0:T(8,128)}), f32[13830,128]{1,0:T(8,128)}) %all-reduce.2.cloned.1.call-update) | async-done | bytes 7080976 | tf_op jit(solution)/shard_map/psum | solution.py:329
  1404.2 7.7 gather_fusion.1
  1417.1 9.0 copy.86
  1426.1 9.0 copy.88
  1435.1 9.0 copy.87
  (270 shorter events, 193.2 us)
Async XLA Ops:
  7.2 7.7 copy-start.35
  7.2 158.7 %all-gather.10.cloned.1.call-start = ((), (), s32[]{:S(2)}) async-start(), calls=%async_computation.10 | async-start | bytes 11953152 | tf_op jit(solution)/shard_map/all_gather | solution.py:141
  10.8 217.5 %all-gather.6.cloned.1.call-start = ((), (), s32[]{:S(2)}) async-start(), calls=%async_computation.4 | async-start | bytes 7864320 | tf_op jit(solution)/shard_map/all_gather | solution.py:147
  11.6 248.4 %all-gather.8.cloned.1.call-start = ((), (), s32[]{:S(2)}) async-start(), calls=%async_computation.6 | async-start | bytes 7864320 | tf_op jit(solution)/shard_map/all_gather | solution.py:204
  12.3 929.1 %reduce-scatter.9.cloned.1.call-start = ((), (), s32[]{:S(2)}) async-start(), calls=%async_computation.7 | async-start | bytes 7864320 | tf_op jit(solution)/shard_map/reduce_scatter | solution.py:269
  214.3 20.6 %copy-start.31 = (f32[768]{0:T(1024)}, f32[768]{0:T(1024)S(1)}, u32[]{:S(2)}) copy-start(f32[768]{0:T(1024)S(1)} %mul.459) | copy-start | bytes 9220
  214.4 20.5 %copy-start.33 = (f32[768]{0:T(1024)}, f32[768]{0:T(1024)S(1)}, u32[]{:S(2)}) copy-start(f32[768]{0:T(1024)S(1)} %mul.475) | copy-start | bytes 9220
  220.0 6.4 copy-start.16
  225.8 6.4 copy-start.17
  228.3 4.7 copy-start.3
  232.2 2.7 copy-start.36
  234.9 7.9 copy-start.30
  242.8 3.9 copy-start.12
  246.9 13.1 copy-start.18
  269.5 3.6 copy-start.11
  269.5 3.8 copy-start.23
  269.5 3.8 copy-start.25
  273.3 2.8 copy-start.29
  273.3 2.8 copy-start.39
  292.1 12.1 copy-start.7
  332.9 12.1 copy-start.7
  373.7 12.1 copy-start.7
  414.5 12.1 copy-start.7
  439.5 3.3 copy-start.1
  502.9 4.5 copy-start
  512.5 9.5 copy-start.2
  522.0 3.3 copy-start.1
  586.3 4.5 copy-start
  596.9 9.5 copy-start.2
  606.4 3.3 copy-start.1
  670.7 4.5 copy-start
  681.3 9.5 copy-start.2
  690.9 3.3 copy-start.1
  755.1 4.5 copy-start
  765.7 9.5 copy-start.2
  775.6 4.1 copy-start.24
  775.6 4.1 copy-start.26
  788.4 9.5 copy-start.9
  799.1 9.3 slice-start
  801.7 6.7 slice-start.1
  806.5 7.2 slice-start.4
  808.4 5.2 slice-start.5
  838.3 129.8 %reduce-scatter.11.cloned.1.call-start = ((), (), s32[]{:S(2)}) async-start(), calls=%async_computation.8 | async-start | bytes 7864320 | tf_op jit(solution)/shard_map/reduce_scatter | solution.py:272
  838.3 35.7 %slice-start.2 = ((s8[6291456]{0:T(1024)(128)(4,1)}), s8[4194304]{0:T(1024)(128)(4,1)S(1)}, s32[]{:S(2)}) async-start(s8[6291456]{0:T(1024)(128)(4,1)} %bitcast.218), calls=%async_computation.14 | async-start | bytes 8388608
  840.6 33.3 %slice-start.3 = ((s8[6291456]{0:T(1024)(128)(4,1)}), s8[2097152]{0:T(1024)(128)(4,1)S(1)}, s32[]{:S(2)}) async-start(s8[6291456]{0:T(1024)(128)(4,1)} %bitcast.218), calls=%async_computation.15 | async-start | bytes 4194304
  840.7 33.3 %copy-start.20 = (bf16[768,768]{1,0:T(8,128)(2,1)S(1)}, bf16[768,768]{1,0:T(8,128)(2,1)}, u32[]{:S(2)}) copy-start(bf16[768,768]{1,0:T(8,128)(2,1)} %reshape.377) | copy-start | bytes 3538948
  883.2 2.6 copy-start.38
  902.2 5.8 copy-start.15
  909.1 91.2 %reduce-scatter.13.cloned.1.call-start = ((), (), s32[]{:S(2)}) async-start(), calls=%async_computation.11 | async-start | bytes 491520
  909.1 6.2 copy-start.10
  917.7 12.2 copy-start.21
  929.9 11.5 copy-start.28
  946.8 30.2 %copy-start.19 = (bf16[192,768]{1,0:T(8,128)(2,1)S(1)}, bf16[192,768]{1,0:T(8,128)(2,1)}, u32[]{:S(2)}) copy-start(bf16[192,768]{1,0:T(8,128)(2,1)} %reshape.375) | copy-start | bytes 884740
  968.1 3.8 copy-start.6
  976.5 262.1 %reduce-scatter.7.cloned.1.call-start = ((), (), s32[]{:S(2)}) async-start(), calls=%async_computation.5 | async-start | bytes 7864320 | tf_op jit(solution)/shard_map/reduce_scatter | solution.py:200
  994.2 410.0 %all-reduce.2.cloned.1.call-start = ((), (), s32[]{:S(2)}) async-start(), calls=%async_computation.9 | async-start | bytes 14163968 | tf_op jit(solution)/shard_map/psum | solution.py:329
  994.3 8.0 copy-start.37
  1050.1 119.3 %copy-start.40 = (f32[2]{0:T(128)}, f32[2]{0:T(128)S(1)}, u32[]{:S(2)}) copy-start(f32[2]{0:T(128)S(1)} %sqrt.7) | copy-start | bytes 28
  1169.4 65.9 %copy-start.5 = (bf16[1024,768]{1,0:T(8,128)(2,1)S(1)}, bf16[1024,768]{1,0:T(8,128)(2,1)}, u32[]{:S(2)}) copy-start(bf16[1024,768]{1,0:T(8,128)(2,1)} %reduce-scatter.9.cloned.1.call-done) | copy-start | bytes 4718596
  1169.4 65.9 %copy-start.32 = (f32[768]{0:T(1024)S(1)}, f32[768]{0:T(1024)}, u32[]{:S(2)}) copy-start(f32[768]{0:T(1024)} %copy-done.31) | copy-start | bytes 9220
  1169.4 65.9 %copy-start.34 = (f32[768]{0:T(1024)S(1)}, f32[768]{0:T(1024)}, u32[]{:S(2)}) copy-start(f32[768]{0:T(1024)} %copy-done.33) | copy-start | bytes 9220
  1235.3 7.0 dynamic-slice-start
  1238.6 3.6 copy-start.13
  1246.7 165.3 %copy-start.14 = (f32[1,2594,128]{2,0,1:T(1,128)S(1)}, f32[1,2594,128]{2,0,1:T(1,128)}, u32[]{:S(2)}) copy-start(f32[1,2594,128]{2,0,1:T(1,128)} %param.15) | copy-start | bytes 3984388
  (7 other events, 9.8 us)
Sparse Core Ops, SparseCore 0:
  10.9 154.8 all-gather.9
  167.4 44.5 all-gather.5
  213.6 46.4 all-gather.7
  838.4 58.8 reduce-scatter.8
  909.2 58.8 reduce-scatter.10
  976.7 20.7 reduce-scatter.12
  1000.0 58.9 reduce-scatter.6
  1169.5 234.6 all-reduce.1
where the time goes:
time: 1460 us; the launch traced here: 1450 us
  matrix products  624 us (43%)
  waiting for transfers between devices  339 us (23%)
  local copies, waits for them, and re-layouts  273 us (19%)
  other arithmetic  172 us (12%)
  loops' own time  16.5 us (1%)
  between operations  15.2 us (1%)
    psum x1, waiting for transfers between devices, on_device(): summed = lax.psum(grad_rows, 'dp')  158 us
    all_gather x1, waiting for transfers between devices, on_device(): lax.all_gather(master[0].astype(jnp.bfloat16), 'dp', axis=0, tiled=True)  149 us
    dot_general x1, matrix products, on_device(): clipped = jnp.dot(clip_scale, group_grads, precision=lax.Precision.HIGHEST)  119 us
    dot_general x8, matrix products, scores_of(): jnp.einsum('sqhd,skhd->shqk', query_block, key_rows, preferred_element_ty...  93.7 us
    unnamed x100, local copies, waits for them, and re-layouts  83.8 us
    dot_general x4, matrix products, backward_block(): jnp.einsum('sqhd,skhd->shqk', grad_block, values, preferred_element_type=...  72.5 us
    convert_element_type x4, other arithmetic, backward_block(): grad_scores = (probs * (grad_probs - row_dot)).astype(jnp.bfloat16)  68.2 us
    scatter x1, local copies, waits for them, and re-layouts, on_device(): slot_block = jnp.full((slot_total,), -1, jnp.int32).at[block_slot].set(jn...  65.6 us
  transfers between devices with their start and end apart: 8, of which 4 were waited for; matrix products, arithmetic and copies ran while one was open for 31% of the time, Pallas kernels for 0%

commit v1 on v0

--- a/solution.py
+++ b/solution.py
@@ -13,6 +13,37 @@
 beta_two = 0.6
 root_half = 0.7071067811865476
 inv_root_tau = 0.3989422804014327
+
+
+def view_tasks(content, dim_at):
+    peer_axis = "dp"
+    current_block, top, built = (
+        lax.axis_size(peer_axis),
+        lax.axis_index(peer_axis),
+        content.shape[dim_at],
+    )
+    slots = tuple(((dev_j, (dev_j + 1) % current_block) for dev_j in range(current_block)))
+    parts_seen = tuple(((dev_j, (dev_j - 1) % current_block) for dev_j in range(current_block)))
+    w2 = jnp.zeros(
+        (*content.shape[:dim_at], current_block * built, *content.shape[dim_at + 1 :]),
+        content.dtype,
+    )
+    w2 = lax.dynamic_update_slice_in_dim(w2, content, top * built, axis=dim_at)
+    f_now = mixed_arr = content
+    ix = 1
+    fresh = current_block // 2
+    while ix < fresh + 1:
+        f_now = lax.ppermute(f_now, peer_axis, slots)
+        w2 = lax.dynamic_update_slice_in_dim(
+            w2, f_now, (top - ix) % current_block * built, axis=dim_at
+        )
+        if ix < current_block - fresh:
+            mixed_arr = lax.ppermute(mixed_arr, peer_axis, parts_seen)
+            w2 = lax.dynamic_update_slice_in_dim(
+                w2, mixed_arr, (top + ix) % current_block * built, axis=dim_at
+            )
+        ix += 1
+    return w2
 
 
 def rotary_tables(length, rot_dims):
@@ -138,7 +169,7 @@
     capacity = master.shape[1]
     block_width = master.shape[2]
     block_count = block_slot.shape[0]
-    copies = lax.all_gather(master[0].astype(jnp.bfloat16), "dp", axis=0, tiled=True)
+    copies = view_tasks(master[0].astype(jnp.bfloat16), 0)
     flat_params = copies[block_slot].reshape(-1)
     w_qkv, w_out, w_up, w_down, norm_local = unpack(
         flat_params, d_model, heads_local, ff_local, width_local

time: 1460 us -> 1410 us (0.966)
  waiting for transfers between devices: 339 us -> 244 us
  local copies, waits for them, and re-layouts: 273 us -> 302 us
  starting transfers between devices: 0.73 us -> 20.1 us
    all_gather x1 -> x0, waiting for transfers between devices: 149 us -> none  [on_device(): lax.all_gather(master[0].astype(jnp.bfloat16), 'dp', axis=0, tiled=True)]
    ppermute x0 -> x7, waiting for transfers between devices: none -> 64 us  [the longest x4 63.9 us: view_tasks(): f_now = lax.ppermute(f_now, peer_axis, slots)]
    dynamic_update_slice x0 -> x8, local copies, waits for them, and re-layouts: none -> 35.4 us  [the longest x4 17.6 us: view_tasks(): lax.dynamic_update_slice_in_dim(w2, f_now, (top - ix) % current_block * b...]
    ppermute x0 -> x7, starting transfers between devices: none -> 19.4 us  [the longest x4 10.5 us: view_tasks(): f_now = lax.ppermute(f_now, peer_axis, slots)]
  transfers between devices with their start and end apart: 8 -> 14, of which waited for: 4 -> 5; matrix products, arithmetic and copies ran while one was open for 31% -> 34% of each run, Pallas kernels for 0% -> 0%
where the time goes in v1:
time: 1410 us; the launch traced here: 1400 us
  matrix products  625 us (44%)
  local copies, waits for them, and re-layouts  302 us (21%)
  waiting for transfers between devices  244 us (17%)
  other arithmetic  168 us (12%)
  starting transfers between devices  20.1 us (1%)
  loops' own time  16.5 us (1%)
  between operations  15.4 us (1%)
    psum x1, waiting for transfers between devices, on_device(): summed = lax.psum(grad_rows, 'dp')  158 us
    dot_general x1, matrix products, on_device(): clipped = jnp.dot(clip_scale, group_grads, precision=lax.Precision.HIGHEST)  119 us
    dot_general x8, matrix products, scores_of(): jnp.einsum('sqhd,skhd->shqk', query_block, key_rows, preferred_element_ty...  93.7 us
    unnamed x100, local copies, waits for them, and re-layouts  76.1 us
    dot_general x4, matrix products, backward_block(): jnp.einsum('sqhd,skhd->shqk', grad_block, values, preferred_element_type=...  72.5 us
    convert_element_type x4, other arithmetic, backward_block(): grad_scores = (probs * (grad_probs - row_dot)).astype(jnp.bfloat16)  68.2 us
    scatter x1, local copies, waits for them, and re-layouts, on_device(): slot_block = jnp.full((slot_total,), -1, jnp.int32).at[block_slot].set(jn...  65.6 us
    ppermute x4, waiting for transfers between devices, view_tasks(): f_now = lax.ppermute(f_now, peer_axis, slots)  63.9 us
  transfers between devices with their start and end apart: 14, of which 5 were waited for; matrix products, arithmetic and copies ran while one was open for 34% of the time, Pallas kernels for 0%

profile of v1, /device:TPU:0, one launch (start us, length us, event | category | flops | bytes accessed | tf_op | source)
XLA Modules:
  0.0 1401.6 jit_solution(11389081949527109156)
XLA Ops:
  15.5 25.4 %collective-permute-done = bf16[2594,128]{1,0:T(8,128)(2,1)S(1)} collective-permute-done((bf16[2594,128]{1,0:T(8,128)(2,1)S(1)}, bf16[2594,128]{1,0:T(8,128)(2,1)S(1)}, u32[]{:S(2)}, u32[]{:S(2)}) %collective-permute-start) | collective-permute-done | bytes 664096 | tf_op jit(solution)/shard_map/ppermute | solution.py:36
  54.9 16.2 %collective-permute-done.2 = bf16[2594,128]{1,0:T(8,128)(2,1)S(1)} collective-permute-done((bf16[2594,128]{1,0:T(8,128)(2,1)S(1)}, bf16[2594,128]{1,0:T(8,128)(2,1)S(1)}, u32[]{:S(2)}, u32[]{:S(2)}) %collective-permute-start.2) | collective-permute-done | bytes 664096 | tf_op jit(solution)/shard_map/ppermute | solution.py:36
  78.0 22.4 %collective-permute-done.4 = bf16[2594,128]{1,0:T(8,128)(2,1)S(1)} collective-permute-done((bf16[2594,128]{1,0:T(8,128)(2,1)S(1)}, bf16[2594,128]{1,0:T(8,128)(2,1)S(1)}, u32[]{:S(2)}, u32[]{:S(2)}) %collective-permute-start.4) | collective-permute-done | bytes 664096 | tf_op jit(solution)/shard_map/ppermute | solution.py:36
  135.4 29.7 %gather_fusion = bf16[13830,128]{1,0:T(8,128)(2,1)S(1)} fusion(bf16[20752,128]{1,0:T(8,128)(2,1)} %dynamic_update_slice.42, s32[14336]{0:T(1024)} %pad_clamp_fusion), kind=kCustom, calls=%fused_computation | custom fusion | bytes 7136280 | tf_op jit(solution)/shard_map/gather | solution.py:173
  194.7 7.9 fusion.36
  209.8 6.1 fusion.55
  225.8 163.2 %while.30 = (s32[]{:T(128)}, bf16[4,2,512,3,64]{2,4,3,1,0:T(8,128)(2,1)}, f32[4,2,3,512,1]{3,2,1,4,0:T(4,128)S(1)}, s32[4]{0:T(128)S(1)}, bf16[2,2048,3,64]{1,3,...) while((s32[]{:T(128)}, ...), condition=%wide.region_5.6_spmd.clone.clone, body=%wide.region_2.5_spmd.clone.sunk.clone | while | flops 1687156224 | bytes 96723152 | solution.py:224
  229.7 12.1 fusion.179
  241.8 12.1 fusion.180
  253.9 11.6 fusion.181
  270.5 12.1 fusion.179
  282.6 12.1 fusion.180
  294.7 11.6 fusion.181
  311.3 12.1 fusion.179
  323.4 12.1 fusion.180
  335.5 11.6 fusion.181
  352.1 12.1 fusion.179
  364.2 12.1 fusion.180
  376.3 11.6 fusion.181
  389.0 336.3 %while.31 = (s32[]{:T(128)}, f32[2,2048,3,64]{1,3,2,0:T(8,128)}, f32[2,2048,3,64]{1,3,2,0:T(8,128)}, f32[4,2,512,3,64]{2,4,3,1,0:T(8,128)}, s32[4]{0:T(128)S(1)}...) while((s32[]{:T(128)}, f32[2,2048,3,64]{1,3,2,0:T(8,128)}, ...), condition=%wide.region_9.10_spmd.clone.clone, body=%wide.region_7.9_spmd.clone.sunk.clone | while | flops 4126078464 | bytes 275603712 | solution.py:280
  393.2 11.3 fusion.191
  404.5 12.9 bitcast_add_fusion.7
  417.4 18.1 %multiply_reduce_fusion.4 = (f32[2,3,512]{2,1,0:T(4,128)S(1)}, f32[2,3,512,2048]{3,2,1,0:T(8,128)}) fusion(f32[2,3,512,2048]{3,2,1,0:T(8,128)} %fusion.191, f32[2,3,512]{2,1,0:T(4,128)S(1)} %dynamic-slice_bitcast_fusion.3, pred[512,2048]{1,0:T(8,128)(4,1)S(1)} %iota_compare_fusion.12, bf16[2,2048,3,64]{1,3,2,0:T(8,128)(2,1)} %copy-done.1, ...), kind=kOutput, calls=%fused_computation.22.clone.1.clone | convolution fusion | flops 836760576 | bytes 53370884 | tf_op jit(solution)/shard_map/while/body/eval_jaxpr/sqhd,skhd->shqk/dot_general | solution.py:255
  435.6 17.0 %multiply_convert_fusion.3 = bf16[2,3,512,2048]{3,2,1,0:T(8,128)(2,1)S(1)} fusion(f32[2,3,512,2048]{3,2,1,0:T(8,128)} %get-tuple-element.403, f32[2,3,512,2048]{3,2,1,0:T(8,128)} %fusion.191, f32[2,3,512]{2,1,0:T(4,128)S(1)} %get-tuple-element.404, f32[2,3,512]{2,1,0:T(4,128)S(1)} %dynamic-slice_bitcast_fusion.3, ...), kind=kLoop, calls=%fused_computation.21.clone.1.clone | loop fusion | flops 37748736 | bytes 63987712 | tf_op jit(solution)/shard_map/while/body/eval_jaxpr/convert_element_type | solution.py:259
  462.2 9.5 fusion.192
  475.7 11.3 fusion.191
  487.0 13.8 bitcast_add_fusion.7
  500.8 18.1 %multiply_reduce_fusion.4 = (f32[2,3,512]{2,1,0:T(4,128)S(1)}, f32[2,3,512,2048]{3,2,1,0:T(8,128)}) fusion(f32[2,3,512,2048]{3,2,1,0:T(8,128)} %fusion.191, f32[2,3,512]{2,1,0:T(4,128)S(1)} %dynamic-slice_bitcast_fusion.3, pred[512,2048]{1,0:T(8,128)(4,1)S(1)} %iota_compare_fusion.12, bf16[2,2048,3,64]{1,3,2,0:T(8,128)(2,1)} %copy-done.1, ...), kind=kOutput, calls=%fused_computation.22.clone.1.clone | convolution fusion | flops 836760576 | bytes 53370884 | tf_op jit(solution)/shard_map/while/body/eval_jaxpr/sqhd,skhd->shqk/dot_general | solution.py:255
  518.9 17.0 %multiply_convert_fusion.3 = bf16[2,3,512,2048]{3,2,1,0:T(8,128)(2,1)S(1)} fusion(f32[2,3,512,2048]{3,2,1,0:T(8,128)} %get-tuple-element.403, f32[2,3,512,2048]{3,2,1,0:T(8,128)} %fusion.191, f32[2,3,512]{2,1,0:T(4,128)S(1)} %get-tuple-element.404, f32[2,3,512]{2,1,0:T(4,128)S(1)} %dynamic-slice_bitcast_fusion.3, ...), kind=kLoop, calls=%fused_computation.21.clone.1.clone | loop fusion | flops 37748736 | bytes 63987712 | tf_op jit(solution)/shard_map/while/body/eval_jaxpr/convert_element_type | solution.py:259
  540.5 6.1 bitcast_add_fusion.6
  546.6 9.6 fusion.192
  560.1 11.3 fusion.191
  571.5 13.8 bitcast_add_fusion.7
  585.3 18.1 %multiply_reduce_fusion.4 = (f32[2,3,512]{2,1,0:T(4,128)S(1)}, f32[2,3,512,2048]{3,2,1,0:T(8,128)}) fusion(f32[2,3,512,2048]{3,2,1,0:T(8,128)} %fusion.191, f32[2,3,512]{2,1,0:T(4,128)S(1)} %dynamic-slice_bitcast_fusion.3, pred[512,2048]{1,0:T(8,128)(4,1)S(1)} %iota_compare_fusion.12, bf16[2,2048,3,64]{1,3,2,0:T(8,128)(2,1)} %copy-done.1, ...), kind=kOutput, calls=%fused_computation.22.clone.1.clone | convolution fusion | flops 836760576 | bytes 53370884 | tf_op jit(solution)/shard_map/while/body/eval_jaxpr/sqhd,skhd->shqk/dot_general | solution.py:255
  603.4 17.0 %multiply_convert_fusion.3 = bf16[2,3,512,2048]{3,2,1,0:T(8,128)(2,1)S(1)} fusion(f32[2,3,512,2048]{3,2,1,0:T(8,128)} %get-tuple-element.403, f32[2,3,512,2048]{3,2,1,0:T(8,128)} %fusion.191, f32[2,3,512]{2,1,0:T(4,128)S(1)} %get-tuple-element.404, f32[2,3,512]{2,1,0:T(4,128)S(1)} %dynamic-slice_bitcast_fusion.3, ...), kind=kLoop, calls=%fused_computation.21.clone.1.clone | loop fusion | flops 37748736 | bytes 63987712 | tf_op jit(solution)/shard_map/while/body/eval_jaxpr/convert_element_type | solution.py:259
  625.0 6.1 bitcast_add_fusion.6
  631.1 9.5 fusion.192
  644.6 11.3 fusion.191
  655.9 13.8 bitcast_add_fusion.7
  669.6 18.1 %multiply_reduce_fusion.4 = (f32[2,3,512]{2,1,0:T(4,128)S(1)}, f32[2,3,512,2048]{3,2,1,0:T(8,128)}) fusion(f32[2,3,512,2048]{3,2,1,0:T(8,128)} %fusion.191, f32[2,3,512]{2,1,0:T(4,128)S(1)} %dynamic-slice_bitcast_fusion.3, pred[512,2048]{1,0:T(8,128)(4,1)S(1)} %iota_compare_fusion.12, bf16[2,2048,3,64]{1,3,2,0:T(8,128)(2,1)} %copy-done.1, ...), kind=kOutput, calls=%fused_computation.22.clone.1.clone | convolution fusion | flops 836760576 | bytes 53370884 | tf_op jit(solution)/shard_map/while/body/eval_jaxpr/sqhd,skhd->shqk/dot_general | solution.py:255
  687.8 17.0 %multiply_convert_fusion.3 = bf16[2,3,512,2048]{3,2,1,0:T(8,128)(2,1)S(1)} fusion(f32[2,3,512,2048]{3,2,1,0:T(8,128)} %get-tuple-element.403, f32[2,3,512,2048]{3,2,1,0:T(8,128)} %fusion.191, f32[2,3,512]{2,1,0:T(4,128)S(1)} %get-tuple-element.404, f32[2,3,512]{2,1,0:T(4,128)S(1)} %dynamic-slice_bitcast_fusion.3, ...), kind=kLoop, calls=%fused_computation.21.clone.1.clone | loop fusion | flops 37748736 | bytes 63987712 | tf_op jit(solution)/shard_map/while/body/eval_jaxpr/convert_element_type | solution.py:259
  715.4 9.5 fusion.192
  738.2 9.5 copy.55
  763.4 9.7 fusion.109
  778.6 9.4 convolution_convert_fusion
  790.4 33.4 %fusion.41 = (bf16[4096,768]{1,0:T(8,128)(2,1)}, f32[4096,768]{1,0:T(8,128)S(1)}) fusion(bf16[4096,768]{1,0:T(8,128)(2,1)} %get-tuple-element.237, bf16[768,768]{1,0:T(8,128)(2,1)S(1)} %copy-done.22), kind=kOutput, calls=%fused_computation.59 | convolution fusion | flops 5036310528 | bytes 26345472 | tf_op jit(solution)/shard_map/dot_general | solution.py:226
  823.8 9.2 fusion.47
  835.5 7.0 convolution_convert_fusion.1
  842.6 9.4 convolution_bitcast_fusion.1
  858.9 6.2 constant_dynamic-update-slice_fusion.2
  867.5 12.3 convolution_bitcast_fusion
  879.9 11.6 fusion.108
  896.8 21.4 %reduce-scatter.11.cloned.1.call-done = bf16[1024,768]{1,0:T(8,128)(2,1)} async-done(((bf16[4096,768]{1,0:T(8,128)(2,1)}), bf16[1024,768]{1,0:T(8,128)(2,1)}) %reduce-scatter.11.cloned.1.call-update) | async-done | bytes 1572880 | tf_op jit(solution)/shard_map/reduce_scatter | solution.py:303
  927.2 9.1 add_convert_fusion
  936.3 8.1 copy.83
  952.5 41.5 %multiply_reduce_fusion.1 = (f32[2]{0:T(128)S(1)}, f32[2,1770240]{1,0:T(2,128)}) fusion(f32[2,1770240]{1,0:T(2,128)} %constant_dynamic-update-slice_fusion, s32[2]{0:T(128)S(1)} %copy-done.37), kind=kOutput, calls=%fused_computation.55 | convolution fusion | flops 92052480 | bytes 28323856 | tf_op jit(solution)/shard_map/dot_general | solution.py:347
  994.0 6.4 psum.14
  1000.4 119.3 %convolution_reduce_fusion = f32[1770240]{0:T(1024)} fusion(f32[2,1770240]{1,0:T(2,128)} %get-tuple-element.257, f32[2]{0:T(128)S(1)} %sqrt.7), kind=kOutput, calls=%fused_computation.115 | convolution fusion | flops 42485764 | bytes 21242888 | tf_op jit(solution)/shard_map/dot_general | solution.py:351
  1119.7 65.6 %scatter_custom_fusion = s32[20752]{0:T(1024)S(1)} fusion(s32[13830]{0:T(1024)} %copy-done.27, s32[13830]{0:T(1024)S(1)} %iota.92, s32[]{:T(128)} %constant.109.clone.1), kind=kCustom, calls=%fused_computation.159 | custom fusion | bytes 83520 | tf_op jit(solution)/shard_map/scatter | solution.py:357
  1196.9 157.6 %all-reduce.2.cloned.1.call-done = f32[13830,128]{1,0:T(8,128)} async-done(((f32[13830,128]{1,0:T(8,128)}), f32[13830,128]{1,0:T(8,128)}) %all-reduce.2.cloned.1.call-update) | async-done | bytes 7080976 | tf_op jit(solution)/shard_map/psum | solution.py:360
  1354.5 7.7 gather_fusion.1
  1367.4 9.0 copy.67
  1376.4 9.0 copy.69
  1385.4 9.0 copy.68
  (289 shorter events, 247.0 us)
Async XLA Ops:
  7.2 181.0 %all-gather.4.cloned.1.call-start = ((), (), s32[]{:S(2)}) async-start(), calls=%async_computation.4 | async-start | bytes 7864320 | tf_op jit(solution)/shard_map/all_gather | solution.py:178
  7.9 201.9 %all-gather.6.cloned.1.call-start = ((), (), s32[]{:S(2)}) async-start(), calls=%async_computation.6 | async-start | bytes 7864320 | tf_op jit(solution)/shard_map/all_gather | solution.py:235
  9.3 65.5 %copy-start.35 = (s32[13830]{0:T(1024)S(1)}, s32[13830]{0:T(1024)}, u32[]{:S(2)}) copy-start(s32[13830]{0:T(1024)} %param.14) | copy-start | bytes 165964
  9.4 31.5 %collective-permute-start = (bf16[2594,128]{1,0:T(8,128)(2,1)S(1)}, bf16[2594,128]{1,0:T(8,128)(2,1)S(1)}, u32[]{:S(2)}, u32[]{:S(2)}) collective-permute-start(bf16[2594,128]{1,0:T(8,128)(2,1)S(1)} %bitcast.229), channel_id=1, source_target_pairs={{0,4},{4,8},{8,12},{12,16},{16,20},{20,24},{24,28},{28,0},{1,5},{5... | collective-permute-start | bytes 1992200 | tf_op jit(solution)/shard_map/ppermute | solution.py:36
  12.4 39.8 %collective-permute-start.1 = (bf16[2594,128]{1,0:T(8,128)(2,1)S(1)}, bf16[2594,128]{1,0:T(8,128)(2,1)S(1)}, u32[]{:S(2)}, u32[]{:S(2)}) collective-permute-start(bf16[2594,128]{1,0:T(8,128)(2,1)S(1)} %bitcast.230), channel_id=1, source_target_pairs={{0,28},{4,0},{8,4},{12,8},{16,12},{20,16},{24,20},{28,24},{1,29},{... | collective-permute-start | bytes 1992200 | tf_op jit(solution)/shard_map/ppermute | solution.py:41
  40.8 30.2 %collective-permute-start.2 = (bf16[2594,128]{1,0:T(8,128)(2,1)S(1)}, bf16[2594,128]{1,0:T(8,128)(2,1)S(1)}, u32[]{:S(2)}, u32[]{:S(2)}) collective-permute-start(bf16[2594,128]{1,0:T(8,128)(2,1)S(1)} %collective-permute-done), channel_id=1, source_target_pairs={{0,4},{4,8},{8,12},{12,16},{16,20},{20,24},{24,28},{28,0},{1,5},{5... | collective-permute-start | bytes 1992200 | tf_op jit(solution)/shard_map/ppermute | solution.py:36
  43.4 848.1 %reduce-scatter.9.cloned.1.call-start = ((), (), s32[]{:S(2)}) async-start(), calls=%async_computation.7 | async-start | bytes 7864320 | tf_op jit(solution)/shard_map/reduce_scatter | solution.py:300
  52.1 22.8 %collective-permute-start.3 = (bf16[2594,128]{1,0:T(8,128)(2,1)S(1)}, bf16[2594,128]{1,0:T(8,128)(2,1)S(1)}, u32[]{:S(2)}, u32[]{:S(2)}) collective-permute-start(bf16[2594,128]{1,0:T(8,128)(2,1)S(1)} %collective-permute-done.1), channel_id=1, source_target_pairs={{0,28},{4,0},{8,4},{12,8},{16,12},{20,16},{24,20},{28,24},{1,29},{... | collective-permute-start | bytes 1992200 | tf_op jit(solution)/shard_map/ppermute | solution.py:41
  71.1 29.3 %collective-permute-start.4 = (bf16[2594,128]{1,0:T(8,128)(2,1)S(1)}, bf16[2594,128]{1,0:T(8,128)(2,1)S(1)}, u32[]{:S(2)}, u32[]{:S(2)}) collective-permute-start(bf16[2594,128]{1,0:T(8,128)(2,1)S(1)} %collective-permute-done.2), channel_id=1, source_target_pairs={{0,4},{4,8},{8,12},{12,16},{16,20},{20,24},{24,28},{28,0},{1,5},{5... | collective-permute-start | bytes 1992200 | tf_op jit(solution)/shard_map/ppermute | solution.py:36
  74.9 28.0 %copy-start.27 = (s32[13830]{0:T(1024)}, s32[13830]{0:T(1024)S(1)}, u32[]{:S(2)}) copy-start(s32[13830]{0:T(1024)S(1)} %compare_select_fusion) | copy-start | bytes 165964
  74.9 51.4 %collective-permute-start.5 = (bf16[2594,128]{1,0:T(8,128)(2,1)S(1)}, bf16[2594,128]{1,0:T(8,128)(2,1)}, u32[]{:S(2)}, u32[]{:S(2)}) collective-permute-start(bf16[2594,128]{1,0:T(8,128)(2,1)S(1)} %collective-permute-done.3), channel_id=1, source_target_pairs={{0,28},{4,0},{8,4},{12,8},{16,12},{20,16},{24,20},{28,24},{1,29},{... | collective-permute-start | bytes 1992200 | tf_op jit(solution)/shard_map/ppermute | solution.py:41
  100.4 30.4 %collective-permute-start.6 = (bf16[2594,128]{1,0:T(8,128)(2,1)S(1)}, bf16[2594,128]{1,0:T(8,128)(2,1)}, u32[]{:S(2)}, u32[]{:S(2)}) collective-permute-start(bf16[2594,128]{1,0:T(8,128)(2,1)S(1)} %collective-permute-done.4), channel_id=1, source_target_pairs={{0,4},{4,8},{8,12},{12,16},{16,20},{20,24},{24,28},{28,0},{1,5},{5... | collective-permute-start | bytes 1992200 | tf_op jit(solution)/shard_map/ppermute | solution.py:36
  174.4 20.3 %copy-start.31 = (f32[768]{0:T(1024)}, f32[768]{0:T(1024)S(1)}, u32[]{:S(2)}) copy-start(f32[768]{0:T(1024)S(1)} %mul.489) | copy-start | bytes 9220
  174.5 20.2 %copy-start.33 = (f32[768]{0:T(1024)}, f32[768]{0:T(1024)S(1)}, u32[]{:S(2)}) copy-start(f32[768]{0:T(1024)S(1)} %mul.505) | copy-start | bytes 9220
  180.1 6.2 copy-start.16
  185.6 6.3 copy-start.17
  188.1 4.6 copy-start.3
  194.7 7.9 copy-start.30
  202.5 3.9 copy-start.12
  219.3 3.6 copy-start.11
  219.3 3.8 copy-start.23
  219.3 3.8 copy-start.25
  241.8 12.1 copy-start.7
  282.6 12.1 copy-start.7
  323.4 12.1 copy-start.7
  364.2 12.1 copy-start.7
  389.2 3.3 copy-start.1
  452.6 4.5 copy-start
  462.2 9.5 copy-start.2
  536.0 4.5 copy-start
  546.6 9.6 copy-start.2
  556.2 3.3 copy-start.1
  620.4 4.5 copy-start
  631.1 9.6 copy-start.2
  704.8 4.5 copy-start
  715.4 9.5 copy-start.2
  725.3 4.1 copy-start.24
  725.3 4.1 copy-start.26
  738.2 9.5 copy-start.9
  748.9 9.3 slice-start
  751.4 6.7 slice-start.1
  756.2 7.2 slice-start.4
  758.2 5.2 slice-start.5
  788.0 130.3 %reduce-scatter.11.cloned.1.call-start = ((), (), s32[]{:S(2)}) async-start(), calls=%async_computation.8 | async-start | bytes 7864320 | tf_op jit(solution)/shard_map/reduce_scatter | solution.py:303
  788.1 35.7 %slice-start.2 = ((s8[6291456]{0:T(1024)(128)(4,1)}), s8[4194304]{0:T(1024)(128)(4,1)S(1)}, s32[]{:S(2)}) async-start(s8[6291456]{0:T(1024)(128)(4,1)} %bitcast.217), calls=%async_computation.13 | async-start | bytes 8388608
  790.4 33.4 %slice-start.3 = ((s8[6291456]{0:T(1024)(128)(4,1)}), s8[2097152]{0:T(1024)(128)(4,1)S(1)}, s32[]{:S(2)}) async-start(s8[6291456]{0:T(1024)(128)(4,1)} %bitcast.217), calls=%async_computation.14 | async-start | bytes 4194304
  790.4 33.4 %copy-start.20 = (bf16[768,768]{1,0:T(8,128)(2,1)S(1)}, bf16[768,768]{1,0:T(8,128)(2,1)}, u32[]{:S(2)}) copy-start(bf16[768,768]{1,0:T(8,128)(2,1)} %reshape.377) | copy-start | bytes 3538948
  852.0 5.8 copy-start.15
  858.9 91.7 %reduce-scatter.13.cloned.1.call-start = ((), (), s32[]{:S(2)}) async-start(), calls=%async_computation.10 | async-start | bytes 491520
  858.9 6.2 copy-start.10
  867.5 12.4 copy-start.21
  879.9 11.6 copy-start.28
  896.8 30.4 %copy-start.19 = (bf16[192,768]{1,0:T(8,128)(2,1)S(1)}, bf16[192,768]{1,0:T(8,128)(2,1)}, u32[]{:S(2)}) copy-start(bf16[192,768]{1,0:T(8,128)(2,1)} %reshape.375) | copy-start | bytes 884740
  918.3 3.8 copy-start.6
  926.8 262.1 %reduce-scatter.7.cloned.1.call-start = ((), (), s32[]{:S(2)}) async-start(), calls=%async_computation.5 | async-start | bytes 7864320 | tf_op jit(solution)/shard_map/reduce_scatter | solution.py:231
  944.4 410.1 %all-reduce.2.cloned.1.call-start = ((), (), s32[]{:S(2)}) async-start(), calls=%async_computation.9 | async-start | bytes 14163968 | tf_op jit(solution)/shard_map/psum | solution.py:360
  944.5 8.0 copy-start.37
  1000.4 119.3 %copy-start.40 = (f32[2]{0:T(128)}, f32[2]{0:T(128)S(1)}, u32[]{:S(2)}) copy-start(f32[2]{0:T(128)S(1)} %sqrt.7) | copy-start | bytes 28
  1119.7 65.9 %copy-start.5 = (bf16[1024,768]{1,0:T(8,128)(2,1)S(1)}, bf16[1024,768]{1,0:T(8,128)(2,1)}, u32[]{:S(2)}) copy-start(bf16[1024,768]{1,0:T(8,128)(2,1)} %reduce-scatter.9.cloned.1.call-done) | copy-start | bytes 4718596
  1119.7 65.9 %copy-start.32 = (f32[768]{0:T(1024)S(1)}, f32[768]{0:T(1024)}, u32[]{:S(2)}) copy-start(f32[768]{0:T(1024)} %copy-done.31) | copy-start | bytes 9220
  1119.7 65.9 %copy-start.34 = (f32[768]{0:T(1024)S(1)}, f32[768]{0:T(1024)}, u32[]{:S(2)}) copy-start(f32[768]{0:T(1024)} %copy-done.33) | copy-start | bytes 9220
  1185.5 7.0 dynamic-slice-start
  1188.9 3.6 copy-start.13
  1196.9 165.3 %copy-start.14 = (f32[1,2594,128]{2,0,1:T(1,128)S(1)}, f32[1,2594,128]{2,0,1:T(1,128)}, u32[]{:S(2)}) copy-start(f32[1,2594,128]{2,0,1:T(1,128)} %param.15) | copy-start | bytes 3984388
  (13 other events, 29.7 us)
Sparse Core Ops, SparseCore 0:
  9.5 49.0 all-gather.3
  60.2 46.3 all-gather.5
  788.1 59.2 reduce-scatter.8
  859.0 59.2 reduce-scatter.10
  926.9 20.8 reduce-scatter.12
  950.1 58.9 reduce-scatter.6
  1119.8 234.6 all-reduce.1
